TPU v7x, 32 devices: a whole 2x2x4 slice. The times are simulated.
32 devices in a mesh: row: 8 (over y, x, core), col: 4 (over z).
Axes of the slice: x: 2, y: 2, z: 4, core: 2. Of those that a mesh axis runs over, the one named last changes fastest.
Arguments:
- hidden_in: bfloat16 [1152, 2048], P('col', 'row'), may hold values from -21 to 21
- state: float32 [128, 2048, 1152], P('col', 'row'), may hold values from -4 to 4
- attn_norm_gain: bfloat16 [2048], replicated, may hold values from 0.099609375 to 1.8984375
- w_query: bfloat16 [2048, 2048], P(None, 'row'), may hold values from -0.125 to 0.125
- w_key: bfloat16 [2048, 2048], P(None, 'row'), may hold values from -0.125 to 0.125
- w_value: bfloat16 [2048, 2048], P(None, 'row'), may hold values from -0.125 to 0.125
- w_gate: bfloat16 [2048, 2048], P(None, 'row'), may hold values from -0.125 to 0.125
- w_decay: bfloat16 [2048, 16], replicated, may hold values from -0.125 to 0.125
- w_beta: bfloat16 [2048, 16], replicated, may hold values from -0.125 to 0.125
- decay_log: float32 [16], replicated, may hold values from -3 to 1.5
- decay_bias: float32 [16], replicated, may hold values from -2 to 1
- head_gain: float32 [128], replicated, may hold values from 0.1 to 1.9
- w_out: bfloat16 [2048, 2048], P('row'), may hold values from -0.125 to 0.125
- final_gain: bfloat16 [2048], P('row'), may hold values from 0.099609375 to 1.8984375
- lm_weight: bfloat16 [2048, 20480], P(None, ('row', 'col')), may hold values from -0.28726213 to 0.28726213
- token_ids: int32 [1152], replicated, may hold values from 0 to 20479
- ref_logprob: float32 [1152], replicated, may hold values from -16 to -6
Outputs:
- new_state: float32 [128, 2048, 1152], P('col', 'row')
- logprob: float32 [1152], replicated
- entropy: float32 [1152], replicated
- kl: float32 [1152], replicated
All inputs are finite; a program needn't handle non-finite values.
Results may differ from a plain program's by a relative error of at most 0.0014.
The roundings to bfloat16 on the way count: a program that leaves them out, or rounds other values in their place, can miss the bound.
Values may be sent and summed in bfloat16 or wider, within the bound.
A program may use at most 128 MiB of HBM per device.

v0:
```python
import jax
import jax.numpy as jnp
from jax import lax
from jax.sharding import PartitionSpec as P

D = 2048
HEADS = 16
DK = 128
DV = 128


def partner_2(block, axis, apart):
    count = lax.axis_size(axis)
    route = []
    for low in range(count):
        high = low | 1 << apart
        if high != low and high < count:
            route += [(low, high), (high, low)]
    return lax.ppermute(block, axis, route)


def project(weight, normed):
    return lax.dot_general(
        weight, normed, (((0,), (1,)), ((), ())), preferred_element_type=jnp.float32
    )


def shift_pairs(count, step):
    return [(source, (source + step) % count) for source in range(count)]


def swap_blocks(blocks, axis):
    count = lax.axis_size(axis)
    me = lax.axis_index(axis)
    result = blocks
    for step in range(1, count):
        sent = lax.dynamic_index_in_dim(blocks, (me + step) % count, 0, keepdims=True)
        got = lax.ppermute(sent, axis, shift_pairs(count, step))
        result = lax.dynamic_update_slice_in_dim(result, got, (me - step) % count, 0)
    return result


def gather_blocks(block, axis):
    count = lax.axis_size(axis)
    me = lax.axis_index(axis)
    result = jnp.zeros((count,) + block.shape, block.dtype)
    result = lax.dynamic_update_slice_in_dim(result, block[None], me, 0)
    for step in range(1, count):
        got = lax.ppermute(block[None], axis, shift_pairs(count, step))
        result = lax.dynamic_update_slice_in_dim(result, got, (me - step) % count, 0)
    return result


def sum_blocks(blocks, axis):
    count = lax.axis_size(axis)
    me = lax.axis_index(axis)
    total = lax.dynamic_index_in_dim(blocks, me, 0, keepdims=False)
    for step in range(1, count):
        sent = lax.dynamic_index_in_dim(blocks, (me + step) % count, 0, keepdims=False)
        total = total + lax.ppermute(sent, axis, shift_pairs(count, step))
    return total


def merge_stats(stats, axis):
    every = lax.all_gather(stats, axis, axis=0, tiled=False)
    top = jnp.max(every[:, 0], axis=0)
    shrink = jnp.exp(every[:, 0] - top[None])
    return jnp.stack(
        [
            top,
            jnp.sum(every[:, 1] * shrink, axis=0),
            jnp.sum(every[:, 2] * shrink, axis=0),
            jnp.sum(every[:, 3], axis=0),
        ]
    )


def per_device(
    hidden_in,
    state,
    attn_norm_gain,
    w_query,
    w_key,
    w_value,
    w_gate,
    w_decay,
    w_beta,
    decay_log,
    decay_bias,
    head_gain,
    w_out,
    final_gain,
    lm_weight,
    token_ids,
    ref_logprob,
):
    highest = lax.Precision.HIGHEST
    row_count = lax.axis_size("row")
    col_count = lax.axis_size("col")
    row_index = lax.axis_index("row")
    col_index = lax.axis_index("col")
    group = max(1, row_count // HEADS)
    local_heads = max(1, HEADS // row_count)
    first_head = row_index // group * local_heads
    value_cols = w_value.shape[1]
    value_part = value_cols // local_heads
    block_rows = hidden_in.shape[0]
    key_rows = state.shape[0]
    batch = state.shape[2]
    vocab_dev = lm_weight.shape[1]
    packed = jnp.concatenate([hidden_in, final_gain[None, :]], axis=0)
    whole = lax.all_gather(packed, "row", axis=1, tiled=True)
    whole_rows = whole[:block_rows]
    whole_gain = whole[block_rows].astype(jnp.float32)
    xfull = whole_rows.astype(jnp.float32)
    normed = (
        xfull
        * lax.rsqrt(jnp.mean(xfull * xfull, axis=1, keepdims=True) + 1e-06)
        * attn_norm_gain.astype(jnp.float32)
    ).astype(jnp.bfloat16)
    raw_pair = jnp.stack([project(w_query, normed), project(w_key, normed)]).astype(jnp.bfloat16)
    raw_pair = lax.optimization_barrier(raw_pair)
    for level in range(group.bit_length() - 1):
        partner = partner_2(raw_pair, "row", level)
        upper = row_index >> level & 1 == 1
        raw_pair = jnp.where(
            upper,
            jnp.concatenate([partner, raw_pair], axis=1),
            jnp.concatenate([raw_pair, partner], axis=1),
        )
    pair_f = raw_pair.astype(jnp.float32).reshape(2, local_heads, DK, block_rows)
    unit_pair = (
        pair_f * lax.rsqrt(jnp.sum(pair_f * pair_f, axis=2, keepdims=True) + 1e-06)
    ).astype(jnp.bfloat16)
    key_blocks = unit_pair.reshape(2, local_heads, col_count, key_rows, block_rows)
    swapped = swap_blocks(jnp.transpose(key_blocks, (2, 0, 1, 3, 4)), "col")
    tiles_qk = jnp.transpose(swapped, (1, 2, 3, 0, 4)).reshape(2, local_heads, key_rows, batch)
    query = tiles_qk[0].astype(jnp.float32)
    key = tiles_qk[1].astype(jnp.float32)
    unit_f = unit_pair.astype(jnp.float32)
    intersection = jnp.sum(unit_f[0] * unit_f[1], axis=1)
    value_t = project(w_value, normed)
    gate_t = project(w_gate, normed)
    decay_in = lax.dynamic_slice_in_dim(project(w_decay, normed), first_head, local_heads, 0)
    beta_in = lax.dynamic_slice_in_dim(project(w_beta, normed), first_head, local_heads, 0)
    rate = jnp.exp(lax.dynamic_slice_in_dim(decay_log, first_head, local_heads, 0))
    bias = lax.dynamic_slice_in_dim(decay_bias, first_head, local_heads, 0)
    alpha_t = jnp.exp(-rate[:, None] * jax.nn.softplus(decay_in + bias[:, None]))
    beta_t = jax.nn.sigmoid(beta_in)
    tiles = state.reshape(key_rows, local_heads, value_part, batch)
    value4 = value_t.reshape(local_heads, value_part, block_rows)
    key_major = jnp.transpose(key, (1, 0, 2))
    responses = jnp.stack(
        [
            jnp.einsum("khvb,hkb->hvb", tiles, key, precision=highest),
            jnp.einsum("khvb,hkb->hvb", tiles, query, precision=highest),
        ]
    )
    responses = responses.reshape(2, local_heads, value_part, col_count, block_rows)
    recall, answer = lax.psum_scatter(
        jnp.transpose(responses, (3, 0, 1, 2, 4)), "col", scatter_dimension=0, tiled=False
    )
    write = beta_t[:, None, :] * (value4 - alpha_t[:, None, :] * recall)
    parts = gather_blocks(
        jnp.concatenate([write.reshape(value_cols, block_rows), alpha_t], axis=0), "col"
    )
    parts = jnp.transpose(parts, (1, 0, 2)).reshape(value_cols + local_heads, batch)
    write_all = parts[:value_cols].reshape(local_heads, value_part, batch)
    alpha_all = parts[value_cols:]
    updated = alpha_all[None, :, None, :] * tiles + key_major[:, :, None, :] * write_all[None]
    readout = alpha_t[:, None, :] * answer + intersection[:, None, :] * write
    power = jnp.sum(readout * readout, axis=1)
    for level in range(group.bit_length() - 1):
        power = power + partner_2(power, "row", level)
    gain_part = lax.dynamic_slice_in_dim(head_gain, row_index % group * value_part, value_part, 0)
    gate4 = gate_t.reshape(local_heads, value_part, block_rows)
    mixed = (
        readout
        * lax.rsqrt(power / DV + 1e-05)[:, None, :]
        * gain_part[None, :, None]
        * jax.nn.silu(gate4)
    )
    mixed_heads = mixed.reshape(value_cols, block_rows).astype(jnp.bfloat16)
    share = -(-block_rows // row_count)
    extra = share * row_count - block_rows
    partial = lax.dot_general(
        mixed_heads, w_out, (((0,), (0,)), ((), ())), preferred_element_type=jnp.float32
    )
    branch = lax.psum_scatter(
        jnp.pad(partial, ((0, extra), (0, 0))).reshape(row_count, share, D),
        "row",
        scatter_dimension=0,
        tiled=False,
    )
    own_rows = lax.dynamic_slice_in_dim(
        jnp.pad(whole_rows, ((0, extra), (0, 0))), row_index * share, share, 0
    )
    hidden = own_rows.astype(jnp.float32) + branch
    energy = jnp.mean(hidden * hidden, axis=1, keepdims=True)
    final = (hidden * lax.rsqrt(energy + 1e-06) * whole_gain[None, :]).astype(jnp.bfloat16)
    tall = lax.all_gather(final, ("col", "row"), axis=0, tiled=True)
    if extra:
        tall = tall.reshape(col_count, share * row_count, D)[:, :block_rows].reshape(batch, D)
    logits = jnp.dot(tall, lm_weight, preferred_element_type=jnp.float32)
    vocab_start = (row_index * col_count + col_index) * vocab_dev
    hits = jnp.arange(vocab_dev, dtype=jnp.int32)[None, :] + vocab_start == token_ids[:, None]
    local_pick = jnp.sum(jnp.where(hits, logits, jnp.zeros_like(logits)), axis=1)
    local_top = jnp.max(logits, axis=1)
    expo = jnp.exp(logits - local_top[:, None])
    local_total = jnp.sum(expo, axis=1)
    local_weighted = jnp.sum(expo * logits, axis=1)
    stats = jnp.stack([local_top, local_total, local_weighted, local_pick])
    top, total, weighted, picked = merge_stats(merge_stats(stats, "col"), "row")
    lse = top + jnp.log(total)
    logprob = picked - lse
    entropy = lse - weighted / total
    gap = jnp.clip(ref_logprob - logprob, -20.0, 20.0)
    kl = jnp.minimum(jnp.exp(gap) - gap - 1.0, 10.0)
    new_state = updated.reshape(key_rows, value_cols, batch)
    return (new_state, logprob, entropy, kl)


def solution(mesh):
    in_specs = (
        P("col", "row"),
        P("col", "row", None),
        P(),
        P(None, "row"),
        P(None, "row"),
        P(None, "row"),
        P(None, "row"),
        P(),
        P(),
        P(),
        P(),
        P(),
        P("row", None),
        P("row"),
        P(None, ("row", "col")),
        P(),
        P(),
    )
    out_specs = (P("col", "row", None), P(), P(), P())
    return jax.shard_map(
        per_device, mesh=mesh, in_specs=in_specs, out_specs=out_specs, check_vma=False
    )
```

profile of v0, /device:TPU:0, one launch (start us, length us, event | category | flops | bytes accessed | tf_op | source)
XLA Modules:
  0.0 320.8 jit_solution(1117575225942106937)
XLA Ops:
  7.2 0.8 broadcast_in_dim.9
  8.0 1.6 pad_maximum_fusion.1
  9.8 0.7 convert_element_type.36
  10.5 26.9 %all-gather.8.cloned.1.call-done = bf16[289,2048]{1,0:T(8,128)(2,1)} async-done(((bf16[289,256]{1,0:T(8,128)(2,1)}), bf16[289,2048]{1,0:T(8,128)(2,1)}) %all-gather.8.cloned.1.call-update) | async-done | bytes 1183760 | tf_op jit(solution)/shard_map/all_gather | solution.py:112
  37.4 1.7 fusion.2
  39.1 1.6 fusion.4
  40.7 0.5 fusion.6
  41.2 0.6 copy-done.1
  41.8 0.6 copy-done.17
  42.4 0.5 fusion.5
  42.9 0.7 copy-done.5
  43.6 1.1 reshape.113
  44.7 1.1 copy.103
  45.9 2.5 multiply_reduce_fusion.3
  48.3 1.1 copy.104
  49.6 1.5 collective-permute-start
  51.2 2.4 collective-permute-start.2
  53.6 0.6 collective-permute-start.1
  54.2 2.9 collective-permute-done
  57.1 5.6 %collective-permute-done.1 = bf16[1,2,2,32,288]{4,3,0,2,1:T(8,128)(2,1)S(1)} collective-permute-done((bf16[1,2,2,32,288]{4,3,0,2,1:T(8,128)(2,1)S(1)}, bf16[1,2,2,32,288]{4,3,0,2,1:T(8,128)(2,1)S(1)}, u32[]{:S(2)}, u32[]{:S(2)}) %collective-permute-start.1) | collective-permute-done | bytes 73760 | tf_op jit(solution)/shard_map/ppermute | solution.py:38
  63.7 0.7 convert_bitcast_fusion
  64.6 17.3 %multiply_reduce_fusion.1 = (f32[2,1152,128]{1,2,0:T(8,128)}, f32[2,1152,128]{1,2,0:T(8,128)}) fusion(f32[2,1152,32,128]{1,3,0,2:T(8,128)} %bitcast.222, f32[2,1152,32]{1,0,2:T(2,128)S(1)} %copy.148, f32[2,1152,32]{1,0,2:T(2,128)S(1)} %copy.149), kind=kLoop, calls=%fused_computation.3 | loop fusion | flops 37158912 | bytes 40697856
  81.9 2.6 copy.130
  84.6 2.7 copy.138
  87.2 1.8 maximum_bitcast_fusion
  89.0 1.6 copy.107
  90.7 0.5 copy-done.18
  91.4 0.9 copy.114
  92.3 1.7 fusion.53
  94.3 2.0 fusion.52
  96.3 0.8 copy.146
  97.1 1.7 fusion.9
  99.3 37.5 %reduce-scatter.3.cloned.1.call-done = f32[1,2,2,128,288]{3,4,2,1,0:T(8,128)} async-done(((f32[4,2,2,128,288]{3,4,2,1,0:T(8,128)}), f32[1,2,2,128,288]{3,4,2,1,0:T(8,128)}) %reduce-scatter.3.cloned.1.call-update) | async-done | bytes 589840 | tf_op jit(solution)/shard_map/reduce_scatter | solution.py:160
  136.8 1.2 fusion.47
  138.0 0.9 copy.113
  140.0 0.5 fusion.15
  140.7 0.5 copy-done.6
  142.5 2.2 fusion.22
  144.8 3.2 %fusion.7 = f32[8,36,2048]{2,1,0:T(8,128)} fusion(bf16[8,36,256]{2,1,0:T(8,128)(2,1)S(1)} %dot_general.55, bf16[256,2048]{1,0:T(8,128)(2,1)} %param.29), kind=kOutput, calls=%fused_computation.19 | convolution fusion | flops 301989888 | bytes 3555328 | tf_op jit(solution)/shard_map/dot_general | solution.py:186
  148.1 2.5 slice.72
  150.6 0.8 slice_convert_fusion
  151.4 39.7 %reduce-scatter.5.cloned.1.call-done = f32[1,36,2048]{2,1,0:T(8,128)} async-done(((f32[8,36,2048]{2,1,0:T(8,128)}), f32[1,36,2048]{2,1,0:T(8,128)}) %reduce-scatter.5.cloned.1.call-update) | async-done | bytes 294928 | tf_op jit(solution)/shard_map/reduce_scatter | solution.py:189
  191.0 1.2 multiply_reduce_fusion.4
  192.3 1.8 fusion.23
  194.1 0.8 maximum_bitcast_fusion.1
  194.9 1.5 collective-permute-start.3
  196.3 2.4 collective-permute-start.4
  198.8 0.9 copy.111
  199.7 1.4 collective-permute-start.5
  201.3 10.6 %collective-permute-done.3 = f32[1,258,288]{1,2,0:T(8,128)} collective-permute-done((f32[1,258,288]{1,2,0:T(8,128)}, f32[1,258,288]{1,2,0:T(8,128)}, u32[]{:S(2)}, u32[]{:S(2)}) %collective-permute-start.3) | collective-permute-done | bytes 297248 | tf_op jit(solution)/shard_map/ppermute | solution.py:49
  211.9 1.0 constant_dynamic-update-slice_fusion.2
  212.9 18.4 %collective-permute-done.4 = f32[1,258,288]{1,2,0:T(8,128)} collective-permute-done((f32[1,258,288]{1,2,0:T(8,128)}, f32[1,258,288]{1,2,0:T(8,128)}, u32[]{:S(2)}, u32[]{:S(2)}) %collective-permute-start.4) | collective-permute-done | bytes 297248 | tf_op jit(solution)/shard_map/ppermute | solution.py:49
  231.3 1.0 constant_dynamic-update-slice_fusion.1
  232.5 1.1 slice.76
  233.6 2.7 copy.112
  236.6 1.2 copy-done.4
  237.8 28.8 %fusion = f32[32,256,1152]{2,1,0:T(8,128)} fusion(f32[32,256,1152]{2,1,0:T(8,128)} %param.18, f32[256,1152]{1,0:T(8,128)S(1)} %copy-done.4, f32[32,2,1152]{2,1,0:T(2,128)S(1)} %copy-done.8, f32[256,1152]{1,0:T(8,128)S(1)} %bitcast.230), kind=kLoop, calls=%fused_computation.1 | loop fusion | flops 28311552 | bytes 78151680 | tf_op jit(solution)/shard_map/add | solution.py:170
  266.6 9.4 %all-gather.10.cloned.1.call-done = bf16[32,36,2048]{2,1,0:T(8,128)(2,1)} async-done(((bf16[1,36,2048]{2,1,0:T(8,128)(2,1)}), bf16[32,36,2048]{2,1,0:T(8,128)(2,1)}) %all-gather.10.cloned.1.call-update) | async-done | bytes 4718608 | tf_op jit(solution)/shard_map/all_gather | solution.py:201
  276.0 7.2 %reshape.120 = bf16[1152,2048]{1,0:T(8,128)(2,1)} reshape(bf16[32,36,2048]{2,1,0:T(8,128)(2,1)} %all-gather.10.cloned.1.call-done) | data formatting | bytes 9437184
  283.2 6.2 %fusion.51 = (f32[1152]{0:T(1024)S(1)}, f32[1152,640]{0,1:T(8,128)S(1)}) fusion(bf16[1152,2048]{1,0:T(8,128)(2,1)} %reshape.120, bf16[2048,640]{1,0:T(8,128)(2,1)S(1)} %copy-done), kind=kOutput, calls=%fused_computation.118 | convolution fusion | flops 3020635136 | bytes 10293760 | tf_op jit(solution)/shard_map/dot_general | solution.py:204
  289.5 0.9 fusion.1
  290.5 13.5 %all-gather.3 = f32[4,4,1152]{2,1,0:T(4,128)S(1)} all-gather(f32[1,4,1152]{2,1,0:T(4,128)S(1)} %maximum_bitcast_fusion.2), channel_id=2, replica_groups=mesh['row'=8,'col'=4] {'col'}, dimensions={0}, use_global_device_ids=true | all-gather | bytes 92160 | tf_op jit(solution)/shard_map/all_gather | solution.py:65
  304.1 9.4 %all-gather.4 = f32[8,4,1152]{2,1,0:T(4,128)S(1)} all-gather(f32[1,4,1152]{2,1,0:T(4,128)S(1)} %maximum_bitcast_fusion.3), channel_id=3, replica_groups=mesh['row'=8,'col'=4] {'row'}, dimensions={0}, use_global_device_ids=true | all-gather | bytes 165888 | tf_op jit(solution)/shard_map/all_gather | solution.py:65
  313.7 0.6 fusion.35
  (102 shorter events, 6.0 us)
Async XLA Ops:
  7.2 276.1 %copy-start = (bf16[2048,640]{1,0:T(8,128)(2,1)S(1)}, bf16[2048,640]{1,0:T(8,128)(2,1)}, u32[]{:S(2)}) copy-start(bf16[2048,640]{1,0:T(8,128)(2,1)} %param.31) | copy-start | bytes 7864324
  7.2 30.2 %all-gather.8.cloned.1.call-start = ((), (), s32[]{:S(2)}) async-start(), calls=%async_computation.2 | async-start | bytes 1363968 | tf_op jit(solution)/shard_map/all_gather | solution.py:112
  9.6 127.2 %reduce-scatter.3.cloned.1.call-start = ((), (), s32[]{:S(2)}) async-start(), calls=%async_computation.3 | async-start | bytes 2949120 | tf_op jit(solution)/shard_map/reduce_scatter | solution.py:160
  37.4 3.3 %copy-start.16 = (bf16[2048,256]{1,0:T(8,128)(2,1)S(1)}, bf16[2048,256]{1,0:T(8,128)(2,1)}, u32[]{:S(2)}) copy-start(bf16[2048,256]{1,0:T(8,128)(2,1)} %param.21) | copy-start | bytes 3145732
  40.7 1.1 copy-start.1
  40.7 1.7 copy-start.17
  42.9 0.7 copy-start.5
  49.6 7.5 %collective-permute-start = (bf16[1,2,2,32,288]{4,3,0,2,1:T(8,128)(2,1)S(1)}, bf16[1,2,2,32,288]{4,3,0,2,1:T(8,128)(2,1)S(1)}, u32[]{:S(2)}, u32[]{:S(2)}) collective-permute-start(bf16[1,2,2,32,288]{4,3,0,2,1:T(8,128)(2,1)S(1)} %get-tuple-element.25), channel_id=1, source_target_pairs={{0,1},{1,2},{2,3},{3,0},{4,5},{5,6},{6,7},{7,4},{8,9},{9,10},{10,1... | collective-permute-start | bytes 221192 | tf_op jit(solution)/shard_map/ppermute | solution.py:38
  51.2 11.5 %collective-permute-start.2 = (bf16[1,2,2,32,288]{4,3,0,2,1:T(8,128)(2,1)S(1)}, bf16[1,2,2,32,288]{4,3,0,2,1:T(8,128)(2,1)S(1)}, u32[]{:S(2)}, u32[]{:S(2)}) collective-permute-start(bf16[1,2,2,32,288]{4,3,0,2,1:T(8,128)(2,1)S(1)} %get-tuple-element.23), channel_id=1, source_target_pairs={{0,3},{1,0},{2,1},{3,2},{4,7},{5,4},{6,5},{7,6},{8,11},{9,8},{10,9... | collective-permute-start | bytes 221192 | tf_op jit(solution)/shard_map/ppermute | solution.py:38
  53.6 9.1 %collective-permute-start.1 = (bf16[1,2,2,32,288]{4,3,0,2,1:T(8,128)(2,1)S(1)}, bf16[1,2,2,32,288]{4,3,0,2,1:T(8,128)(2,1)S(1)}, u32[]{:S(2)}, u32[]{:S(2)}) collective-permute-start(bf16[1,2,2,32,288]{4,3,0,2,1:T(8,128)(2,1)S(1)} %get-tuple-element.24), channel_id=1, source_target_pairs={{0,2},{1,3},{2,0},{3,1},{4,6},{5,7},{6,4},{7,5},{8,10},{9,11},{10,... | collective-permute-start | bytes 221192 | tf_op jit(solution)/shard_map/ppermute | solution.py:38
  90.6 0.7 copy-start.18
  90.6 0.7 copy-start.19
  90.6 0.8 copy-start.20
  90.6 1.7 copy-start.12
  90.6 3.7 %copy-start.13 = (bf16[2048,16]{0,1:T(8,128)(2,1)S(1)}, bf16[2048,16]{0,1:T(8,128)(2,1)}, u32[]{:S(2)}) copy-start(bf16[2048,16]{0,1:T(8,128)(2,1)} %param.25) | copy-start | bytes 196612
  90.6 6.5 %copy-start.3 = (f32[2,2,128,288]{2,1,3,0:T(2,128)S(1)}, f32[2,2,128,288]{2,1,3,0:T(2,128)}, u32[]{:S(2)}) copy-start(f32[2,2,128,288]{2,1,3,0:T(2,128)} %reshape.113) | copy-start | bytes 1769476
  90.7 100.4 %reduce-scatter.5.cloned.1.call-start = ((), (), s32[]{:S(2)}) async-start(), calls=%async_computation.4 | async-start | bytes 2949120 | tf_op jit(solution)/shard_map/reduce_scatter | solution.py:189
  98.8 40.4 %copy-start.11 = (f32[2,288]{0,1:T(8,128)S(1)}, f32[2,288]{0,1:T(8,128)}, u32[]{:S(2)}) copy-start(f32[2,288]{0,1:T(8,128)} %copy.146) | copy-start | bytes 6916
  136.8 3.2 copy-start.2
  136.8 3.2 copy-start.10
  140.0 0.7 copy-start.7
  140.0 1.2 copy-start.6
  148.0 128.0 %all-gather.10.cloned.1.call-start = ((), (), s32[]{:S(2)}) async-start(), calls=%async_computation.5 | async-start | bytes 5406720 | tf_op jit(solution)/shard_map/all_gather | solution.py:201
  148.1 50.7 %copy-start.9 = (f32[32,2,1152]{2,0,1:T(8,128)S(1)}, f32[32,2,1152]{2,0,1:T(8,128)}, u32[]{:S(2)}) copy-start(f32[32,2,1152]{2,0,1:T(8,128)} %get-tuple-element.31) | copy-start | bytes 884740
  194.9 17.0 %collective-permute-start.3 = (f32[1,258,288]{1,2,0:T(8,128)}, f32[1,258,288]{1,2,0:T(8,128)}, u32[]{:S(2)}, u32[]{:S(2)}) collective-permute-start(f32[1,258,288]{1,2,0:T(8,128)} %maximum_bitcast_fusion.1), channel_id=1, source_target_pairs={{0,1},{1,2},{2,3},{3,0},{4,5},{5,6},{6,7},{7,4},{8,9},{9,10},{10,1... | collective-permute-start | bytes 891656 | tf_op jit(solution)/shard_map/ppermute | solution.py:49
  196.3 35.0 %collective-permute-start.4 = (f32[1,258,288]{1,2,0:T(8,128)}, f32[1,258,288]{1,2,0:T(8,128)}, u32[]{:S(2)}, u32[]{:S(2)}) collective-permute-start(f32[1,258,288]{1,2,0:T(8,128)} %maximum_bitcast_fusion.1), channel_id=1, source_target_pairs={{0,2},{1,3},{2,0},{3,1},{4,6},{5,7},{6,4},{7,5},{8,10},{9,11},{10,... | collective-permute-start | bytes 891656 | tf_op jit(solution)/shard_map/ppermute | solution.py:49
  199.7 32.6 %collective-permute-start.5 = (f32[1,258,288]{1,2,0:T(8,128)}, f32[1,258,288]{1,2,0:T(8,128)S(1)}, u32[]{:S(2)}, u32[]{:S(2)}) collective-permute-start(f32[1,258,288]{1,2,0:T(8,128)} %maximum_bitcast_fusion.1), channel_id=1, source_target_pairs={{0,3},{1,0},{2,1},{3,2},{4,7},{5,4},{6,5},{7,6},{8,11},{9,8},{10,9... | collective-permute-start | bytes 891656 | tf_op jit(solution)/shard_map/ppermute | solution.py:49
  233.6 3.0 copy-start.8
  236.5 1.3 copy-start.4
  283.2 6.2 %copy-start.14 = (s32[1152]{0:T(1024)S(1)}, s32[1152]{0:T(1024)}, u32[]{:S(2)}) copy-start(s32[1152]{0:T(1024)} %param.32) | copy-start | bytes 13828
  289.5 24.2 %copy-start.15 = (f32[1152]{0:T(1024)S(1)}, f32[1152]{0:T(1024)}, u32[]{:S(2)}) copy-start(f32[1152]{0:T(1024)} %param.33) | copy-start | bytes 13828
Sparse Core Ops, SparseCore 0:
  10.4 26.9 all-gather.7
  90.8 45.9 reduce-scatter.2
  148.2 42.8 reduce-scatter.4
  194.2 81.7 all-gather.9
where the time goes:
time: 322 us; the launch traced here: 321 us
  waiting for transfers between devices  151 us (47%)
  other arithmetic  66.1 us (21%)
  local copies, waits for them, and re-layouts  39.7 us (12%)
  blocking collectives  22.8 us (7%)
  matrix products  16.8 us (5%)
  between operations  14.4 us (4%)
  starting transfers between devices  10 us (3%)
    reduce_scatter x1, waiting for transfers between devices, per_device(): lax.psum_scatter(jnp.pad(partial, ((0, extra), (0, 0))).reshape(row_count...  39.7 us
    reduce_scatter x1, waiting for transfers between devices, per_device(): lax.psum_scatter(jnp.transpose(responses, (3, 0, 1, 2, 4)), 'col', scatte...  37.5 us
    ppermute x3, waiting for transfers between devices, gather_blocks(): got = lax.ppermute(block[None], axis, shift_pairs(count, step))  29 us
    add x1, other arithmetic, per_device(): alpha_all[None, :, None, :] * tiles  28.8 us
    all_gather x1, waiting for transfers between devices, per_device(): whole = lax.all_gather(packed, 'row', axis=1, tiled=True)  26.9 us
    all_gather x2, blocking collectives, merge_stats(): every = lax.all_gather(stats, axis, axis=0, tiled=False)  22.8 us
    unnamed x5, other arithmetic  19.2 us
    unnamed x47, local copies, waits for them, and re-layouts  13 us
  transfers between devices with their start and end apart: 10, of which 8 were waited for; matrix products, arithmetic and copies ran while one was open for 15% of the time, Pallas kernels for 0%

commit v1 on v0

--- a/solution.py
+++ b/solution.py
@@ -109,7 +109,8 @@
     batch = state.shape[2]
     vocab_dev = lm_weight.shape[1]
     packed = jnp.concatenate([hidden_in, final_gain[None, :]], axis=0)
-    whole = lax.all_gather(packed, "row", axis=1, tiled=True)
+    pieces = lax.all_gather(packed, "row", axis=0, tiled=False)
+    whole = jnp.concatenate(pieces, axis=1)
     whole_rows = whole[:block_rows]
     whole_gain = whole[block_rows].astype(jnp.float32)
     xfull = whole_rows.astype(jnp.float32)

time: 322 us -> 324 us (level)
    unnamed x47 -> x50, local copies, waits for them, and re-layouts: 13 us -> 15.6 us
    unnamed x5 -> x6, other arithmetic: 19.2 us -> 20.7 us
  transfers between devices with their start and end apart: 10 -> 10, of which waited for: 8 -> 8; matrix products, arithmetic and copies ran while one was open for 15% -> 14% of each run, Pallas kernels for 0% -> 0%
where the time goes in v1:
time: 324 us; the launch traced here: 322 us
  waiting for transfers between devices  153 us (47%)
  other arithmetic  64.8 us (20%)
  local copies, waits for them, and re-layouts  40 us (12%)
  blocking collectives  22.8 us (7%)
  matrix products  16.7 us (5%)
  between operations  14.4 us (4%)
  starting transfers between devices  10 us (3%)
    reduce_scatter x1, waiting for transfers between devices, per_device(): lax.psum_scatter(jnp.pad(partial, ((0, extra), (0, 0))).reshape(row_count...  42.2 us
    reduce_scatter x1, waiting for transfers between devices, per_device(): lax.psum_scatter(jnp.transpose(responses, (3, 0, 1, 2, 4)), 'col', scatte...  37.5 us
    ppermute x3, waiting for transfers between devices, gather_blocks(): got = lax.ppermute(block[None], axis, shift_pairs(count, step))  28.9 us
    add x1, other arithmetic, per_device(): alpha_all[None, :, None, :] * tiles  28.8 us
    all_gather x1, waiting for transfers between devices, per_device(): pieces = lax.all_gather(packed, 'row', axis=0, tiled=False)  26.8 us
    all_gather x2, blocking collectives, merge_stats(): every = lax.all_gather(stats, axis, axis=0, tiled=False)  22.8 us
    unnamed x6, other arithmetic  20.7 us
    unnamed x50, local copies, waits for them, and re-layouts  15.6 us
  transfers between devices with their start and end apart: 10, of which 8 were waited for; matrix products, arithmetic and copies ran while one was open for 14% of the time, Pallas kernels for 0%

profile of v1, /device:TPU:0, one launch (start us, length us, event | category | flops | bytes accessed | tf_op | source)
XLA Modules:
  0.0 322.2 jit_solution(15305132336633405148)
XLA Ops:
  7.2 0.8 broadcast_in_dim.9
  8.0 1.6 maximum_bitcast_fusion.2
  9.8 0.7 convert_element_type.48
  10.5 26.8 %all-gather.10.cloned.1.call-done = bf16[8,289,256]{2,1,0:T(8,128)(2,1)} async-done(((bf16[1,289,256]{2,1,0:T(8,128)(2,1)}), bf16[8,289,256]{2,1,0:T(8,128)(2,1)}) %all-gather.10.cloned.1.call-update) | async-done | bytes 1183760 | tf_op jit(solution)/shard_map/all_gather | solution.py:112
  37.3 1.6 multiply_reduce_fusion.3
  38.8 1.3 slice_bitcast_fusion
  40.7 1.3 copy-done.17
  42.0 0.5 fusion.3
  42.5 0.5 copy-done.1
  43.0 0.6 copy-done.18
  43.7 0.5 fusion.2
  44.2 0.7 copy-done.6
  44.9 1.1 reshape.128
  46.0 1.1 copy.109
  47.2 2.5 multiply_reduce_fusion.4
  49.6 1.1 copy.110
  50.9 1.5 collective-permute-start
  52.5 2.4 collective-permute-start.2
  54.9 0.6 collective-permute-start.1
  55.5 2.9 collective-permute-done
  58.4 5.6 %collective-permute-done.1 = bf16[1,2,2,32,288]{4,3,0,2,1:T(8,128)(2,1)S(1)} collective-permute-done((bf16[1,2,2,32,288]{4,3,0,2,1:T(8,128)(2,1)S(1)}, bf16[1,2,2,32,288]{4,3,0,2,1:T(8,128)(2,1)S(1)}, u32[]{:S(2)}, u32[]{:S(2)}) %collective-permute-start.1) | collective-permute-done | bytes 73760 | tf_op jit(solution)/shard_map/ppermute | solution.py:38
  64.9 0.8 convert_bitcast_fusion
  65.9 17.3 %multiply_reduce_fusion.1 = (f32[2,1152,128]{1,2,0:T(8,128)}, f32[2,1152,128]{1,2,0:T(8,128)}) fusion(f32[2,1152,32,128]{1,3,0,2:T(8,128)} %bitcast.228, f32[2,1152,32]{1,0,2:T(2,128)S(1)} %copy.154, f32[2,1152,32]{1,0,2:T(2,128)S(1)} %copy.155), kind=kLoop, calls=%fused_computation.3 | loop fusion | flops 37158912 | bytes 40697856
  83.2 2.7 copy.136
  85.9 2.7 copy.144
  88.6 1.8 maximum_bitcast_fusion
  90.4 1.6 copy.113
  92.0 0.5 copy-done.19
  92.7 0.9 copy.120
  93.6 1.7 fusion.50
  95.6 2.0 fusion.49
  97.6 0.8 copy.152
  98.4 1.7 fusion.6
  100.6 37.5 %reduce-scatter.3.cloned.1.call-done = f32[1,2,2,128,288]{3,4,2,1,0:T(8,128)} async-done(((f32[4,2,2,128,288]{3,4,2,1,0:T(8,128)}), f32[1,2,2,128,288]{3,4,2,1,0:T(8,128)}) %reduce-scatter.3.cloned.1.call-update) | async-done | bytes 589840 | tf_op jit(solution)/shard_map/reduce_scatter | solution.py:161
  138.1 1.2 fusion.44
  139.3 0.9 copy.119
  141.3 0.5 fusion.12
  142.0 0.5 copy-done.7
  143.8 2.2 fusion.19
  146.1 3.2 %fusion.4 = f32[8,36,2048]{2,1,0:T(8,128)} fusion(bf16[8,36,256]{2,1,0:T(8,128)(2,1)S(1)} %dot_general.55, bf16[256,2048]{1,0:T(8,128)(2,1)} %param.29), kind=kOutput, calls=%fused_computation.16 | convolution fusion | flops 301989888 | bytes 3555328 | tf_op jit(solution)/shard_map/dot_general | solution.py:187
  149.4 0.8 slice_convert_fusion
  150.2 42.2 %reduce-scatter.5.cloned.1.call-done = f32[1,36,2048]{2,1,0:T(8,128)} async-done(((f32[8,36,2048]{2,1,0:T(8,128)}), f32[1,36,2048]{2,1,0:T(8,128)}) %reduce-scatter.5.cloned.1.call-update) | async-done | bytes 294928 | tf_op jit(solution)/shard_map/reduce_scatter | solution.py:190
  192.4 1.2 multiply_reduce_fusion.5
  193.6 1.8 fusion.20
  195.4 0.8 maximum_bitcast_fusion.1
  196.2 1.5 collective-permute-start.3
  197.7 2.4 collective-permute-start.4
  200.1 0.9 copy.117
  201.0 1.4 collective-permute-start.5
  202.6 10.5 %collective-permute-done.3 = f32[1,258,288]{1,2,0:T(8,128)} collective-permute-done((f32[1,258,288]{1,2,0:T(8,128)}, f32[1,258,288]{1,2,0:T(8,128)}, u32[]{:S(2)}, u32[]{:S(2)}) %collective-permute-start.3) | collective-permute-done | bytes 297248 | tf_op jit(solution)/shard_map/ppermute | solution.py:49
  213.1 1.0 constant_dynamic-update-slice_fusion.2
  214.2 18.4 %collective-permute-done.4 = f32[1,258,288]{1,2,0:T(8,128)} collective-permute-done((f32[1,258,288]{1,2,0:T(8,128)}, f32[1,258,288]{1,2,0:T(8,128)}, u32[]{:S(2)}, u32[]{:S(2)}) %collective-permute-start.4) | collective-permute-done | bytes 297248 | tf_op jit(solution)/shard_map/ppermute | solution.py:49
  232.6 1.0 constant_dynamic-update-slice_fusion.1
  233.8 1.1 slice.81
  234.9 2.7 copy.118
  237.9 1.2 copy-done.5
  239.1 28.8 %fusion = f32[32,256,1152]{2,1,0:T(8,128)} fusion(f32[32,256,1152]{2,1,0:T(8,128)} %param.18, f32[256,1152]{1,0:T(8,128)S(1)} %copy-done.5, f32[32,2,1152]{2,1,0:T(2,128)S(1)} %copy-done.9, f32[256,1152]{1,0:T(8,128)S(1)} %bitcast.239), kind=kLoop, calls=%fused_computation.1 | loop fusion | flops 28311552 | bytes 78151680 | tf_op jit(solution)/shard_map/add | solution.py:171
  267.9 9.4 %all-gather.12.cloned.1.call-done = bf16[32,36,2048]{2,1,0:T(8,128)(2,1)} async-done(((bf16[1,36,2048]{2,1,0:T(8,128)(2,1)}), bf16[32,36,2048]{2,1,0:T(8,128)(2,1)}) %all-gather.12.cloned.1.call-update) | async-done | bytes 4718608 | tf_op jit(solution)/shard_map/all_gather | solution.py:202
  277.3 7.2 %reshape.138 = bf16[1152,2048]{1,0:T(8,128)(2,1)} reshape(bf16[32,36,2048]{2,1,0:T(8,128)(2,1)} %all-gather.12.cloned.1.call-done) | data formatting | bytes 9437184
  284.6 6.2 %fusion.48 = (f32[1152]{0:T(1024)S(1)}, f32[1152,640]{0,1:T(8,128)S(1)}) fusion(bf16[1152,2048]{1,0:T(8,128)(2,1)} %reshape.138, bf16[2048,640]{1,0:T(8,128)(2,1)S(1)} %copy-done), kind=kOutput, calls=%fused_computation.116 | convolution fusion | flops 3020635136 | bytes 10293760 | tf_op jit(solution)/shard_map/dot_general | solution.py:205
  290.8 0.9 fusion.1
  291.8 13.5 %all-gather.5 = f32[4,4,1152]{2,1,0:T(4,128)S(1)} all-gather(f32[1,4,1152]{2,1,0:T(4,128)S(1)} %maximum_bitcast_fusion.3), channel_id=3, replica_groups=mesh['row'=8,'col'=4] {'col'}, dimensions={0}, use_global_device_ids=true | all-gather | bytes 92160 | tf_op jit(solution)/shard_map/all_gather | solution.py:65
  305.5 9.3 %all-gather.6 = f32[8,4,1152]{2,1,0:T(4,128)S(1)} all-gather(f32[1,4,1152]{2,1,0:T(4,128)S(1)} %maximum_bitcast_fusion.4), channel_id=4, replica_groups=mesh['row'=8,'col'=4] {'row'}, dimensions={0}, use_global_device_ids=true | all-gather | bytes 165888 | tf_op jit(solution)/shard_map/all_gather | solution.py:65
  315.0 0.6 fusion.32
  (105 shorter events, 6.5 us)
Async XLA Ops:
  7.2 277.4 %copy-start = (bf16[2048,640]{1,0:T(8,128)(2,1)S(1)}, bf16[2048,640]{1,0:T(8,128)(2,1)}, u32[]{:S(2)}) copy-start(bf16[2048,640]{1,0:T(8,128)(2,1)} %param.31) | copy-start | bytes 7864324
  7.2 30.1 %all-gather.10.cloned.1.call-start = ((), (), s32[]{:S(2)}) async-start(), calls=%async_computation.4 | async-start | bytes 1363968 | tf_op jit(solution)/shard_map/all_gather | solution.py:112
  9.6 128.5 %reduce-scatter.3.cloned.1.call-start = ((), (), s32[]{:S(2)}) async-start(), calls=%async_computation.2 | async-start | bytes 2949120 | tf_op jit(solution)/shard_map/reduce_scatter | solution.py:161
  40.4 2.2 copy-start.3
  40.4 1.7 copy-start.17
  42.0 1.0 copy-start.1
  42.0 1.7 copy-start.18
  44.2 0.7 copy-start.6
  50.9 7.5 %collective-permute-start = (bf16[1,2,2,32,288]{4,3,0,2,1:T(8,128)(2,1)S(1)}, bf16[1,2,2,32,288]{4,3,0,2,1:T(8,128)(2,1)S(1)}, u32[]{:S(2)}, u32[]{:S(2)}) collective-permute-start(bf16[1,2,2,32,288]{4,3,0,2,1:T(8,128)(2,1)S(1)} %get-tuple-element.25), channel_id=1, source_target_pairs={{0,1},{1,2},{2,3},{3,0},{4,5},{5,6},{6,7},{7,4},{8,9},{9,10},{10,1... | collective-permute-start | bytes 221192 | tf_op jit(solution)/shard_map/ppermute | solution.py:38
  52.5 11.5 %collective-permute-start.2 = (bf16[1,2,2,32,288]{4,3,0,2,1:T(8,128)(2,1)S(1)}, bf16[1,2,2,32,288]{4,3,0,2,1:T(8,128)(2,1)S(1)}, u32[]{:S(2)}, u32[]{:S(2)}) collective-permute-start(bf16[1,2,2,32,288]{4,3,0,2,1:T(8,128)(2,1)S(1)} %get-tuple-element.23), channel_id=1, source_target_pairs={{0,3},{1,0},{2,1},{3,2},{4,7},{5,4},{6,5},{7,6},{8,11},{9,8},{10,9... | collective-permute-start | bytes 221192 | tf_op jit(solution)/shard_map/ppermute | solution.py:38
  54.9 9.1 %collective-permute-start.1 = (bf16[1,2,2,32,288]{4,3,0,2,1:T(8,128)(2,1)S(1)}, bf16[1,2,2,32,288]{4,3,0,2,1:T(8,128)(2,1)S(1)}, u32[]{:S(2)}, u32[]{:S(2)}) collective-permute-start(bf16[1,2,2,32,288]{4,3,0,2,1:T(8,128)(2,1)S(1)} %get-tuple-element.24), channel_id=1, source_target_pairs={{0,2},{1,3},{2,0},{3,1},{4,6},{5,7},{6,4},{7,5},{8,10},{9,11},{10,... | collective-permute-start | bytes 221192 | tf_op jit(solution)/shard_map/ppermute | solution.py:38
  91.9 0.7 copy-start.19
  91.9 0.7 copy-start.20
  91.9 0.8 copy-start.21
  91.9 1.7 copy-start.13
  91.9 3.6 %copy-start.14 = (bf16[2048,16]{0,1:T(8,128)(2,1)S(1)}, bf16[2048,16]{0,1:T(8,128)(2,1)}, u32[]{:S(2)}) copy-start(bf16[2048,16]{0,1:T(8,128)(2,1)} %param.25) | copy-start | bytes 196612
  92.0 6.5 %copy-start.4 = (f32[2,2,128,288]{2,1,3,0:T(2,128)S(1)}, f32[2,2,128,288]{2,1,3,0:T(2,128)}, u32[]{:S(2)}) copy-start(f32[2,2,128,288]{2,1,3,0:T(2,128)} %reshape.128) | copy-start | bytes 1769476
  92.0 100.4 %reduce-scatter.5.cloned.1.call-start = ((), (), s32[]{:S(2)}) async-start(), calls=%async_computation.3 | async-start | bytes 2949120 | tf_op jit(solution)/shard_map/reduce_scatter | solution.py:190
  100.1 40.4 %copy-start.12 = (f32[2,288]{0,1:T(8,128)S(1)}, f32[2,288]{0,1:T(8,128)}, u32[]{:S(2)}) copy-start(f32[2,288]{0,1:T(8,128)} %copy.152) | copy-start | bytes 6916
  138.1 3.2 copy-start.2
  138.1 3.2 copy-start.11
  141.3 0.7 copy-start.8
  141.3 1.2 copy-start.7
  149.3 50.7 %copy-start.10 = (f32[32,2,1152]{2,0,1:T(8,128)S(1)}, f32[32,2,1152]{2,0,1:T(8,128)}, u32[]{:S(2)}) copy-start(f32[32,2,1152]{2,0,1:T(8,128)} %get-tuple-element.31) | copy-start | bytes 884740
  149.3 128.0 %all-gather.12.cloned.1.call-start = ((), (), s32[]{:S(2)}) async-start(), calls=%async_computation.5 | async-start | bytes 5406720 | tf_op jit(solution)/shard_map/all_gather | solution.py:202
  196.2 17.0 %collective-permute-start.3 = (f32[1,258,288]{1,2,0:T(8,128)}, f32[1,258,288]{1,2,0:T(8,128)}, u32[]{:S(2)}, u32[]{:S(2)}) collective-permute-start(f32[1,258,288]{1,2,0:T(8,128)} %maximum_bitcast_fusion.1), channel_id=1, source_target_pairs={{0,1},{1,2},{2,3},{3,0},{4,5},{5,6},{6,7},{7,4},{8,9},{9,10},{10,1... | collective-permute-start | bytes 891656 | tf_op jit(solution)/shard_map/ppermute | solution.py:49
  197.7 34.9 %collective-permute-start.4 = (f32[1,258,288]{1,2,0:T(8,128)}, f32[1,258,288]{1,2,0:T(8,128)}, u32[]{:S(2)}, u32[]{:S(2)}) collective-permute-start(f32[1,258,288]{1,2,0:T(8,128)} %maximum_bitcast_fusion.1), channel_id=1, source_target_pairs={{0,2},{1,3},{2,0},{3,1},{4,6},{5,7},{6,4},{7,5},{8,10},{9,11},{10,... | collective-permute-start | bytes 891656 | tf_op jit(solution)/shard_map/ppermute | solution.py:49
  201.0 32.6 %collective-permute-start.5 = (f32[1,258,288]{1,2,0:T(8,128)}, f32[1,258,288]{1,2,0:T(8,128)S(1)}, u32[]{:S(2)}, u32[]{:S(2)}) collective-permute-start(f32[1,258,288]{1,2,0:T(8,128)} %maximum_bitcast_fusion.1), channel_id=1, source_target_pairs={{0,3},{1,0},{2,1},{3,2},{4,7},{5,4},{6,5},{7,6},{8,11},{9,8},{10,9... | collective-permute-start | bytes 891656 | tf_op jit(solution)/shard_map/ppermute | solution.py:49
  234.9 3.0 copy-start.9
  237.8 1.3 copy-start.5
  284.6 6.2 %copy-start.15 = (s32[1152]{0:T(1024)S(1)}, s32[1152]{0:T(1024)}, u32[]{:S(2)}) copy-start(s32[1152]{0:T(1024)} %param.32) | copy-start | bytes 13828
  290.8 24.2 %copy-start.16 = (f32[1152]{0:T(1024)S(1)}, f32[1152]{0:T(1024)}, u32[]{:S(2)}) copy-start(f32[1152]{0:T(1024)} %param.33) | copy-start | bytes 13828
Sparse Core Ops, SparseCore 0:
  10.4 26.7 all-gather.9
  92.1 45.9 reduce-scatter.2
  149.5 42.8 reduce-scatter.4
  195.5 81.7 all-gather.11
